TPU v7x, 32 devices: a whole 2x2x4 slice. The times are simulated.
32 devices in a mesh: tm: 2 (over core), rows: 16 (over z, y, x).
Axes of the slice: x: 2, y: 2, z: 4, core: 2. Of those that a mesh axis runs over, the one named last changes fastest.
Arguments:
- tiles: bfloat16 [2, 128, 128, 128], P('tm', 'rows'), may hold values from -0.125 to 0.125
- tile_cols: int32 [2, 128], P('tm', 'rows'), may hold values from 0 to 15, as said below
- tile_count: int32 [2, 16], P('tm', 'rows'), may hold values from 4 to 8, as said below
- start_right: bfloat16 [2, 2048, 256], P('tm', 'rows'), may hold values from -48 to 48
Outputs:
- left_embed: float32 [2048, 256], P('rows')
- right_embed: float32 [2, 2048, 256], P('tm', 'rows')
Inputs may be any that keep to these rules, and one draw needn't show every extreme that they name: `tile_cols`: within one row block of one snapshot the 8 slots name distinct column blocks. `tile_count`: some row block of some snapshot has all 8 slots live in every draw.
All inputs are finite; a program needn't handle non-finite values.
Results may differ from a plain program's by a relative error of at most 0.0027.
Values may be sent and summed in bfloat16 or wider, within the bound.
A program may use at most 64 MiB of HBM per device.

v0:
```python
import math
import jax
import jax.numpy as jnp
from jax import lax
from jax.sharding import PartitionSpec as P

BLOCK = 128
COLS = 256


def orthonormal(values, gram, total):
    factor = jnp.linalg.cholesky(gram)
    solved = lax.linalg.triangular_solve(
        factor, values, left_side=False, lower=True, transpose_a=True
    )
    return solved * math.sqrt(total)


def gram_of(values):
    return jnp.dot(values.T, values, precision=lax.Precision.HIGHEST)


def on_device(tiles, tile_cols, tile_count, start_right):
    nrows = lax.axis_size("rows")
    nsnaps = lax.axis_size("tm")
    nodes = BLOCK * nrows
    my_tiles = tiles[0]
    columns = tile_cols[0]
    slot_total = my_tiles.shape[0]
    live = jnp.arange(slot_total, dtype=jnp.int32) < tile_count[0, 0]
    masked = jnp.where(live[:, None, None], my_tiles, jnp.zeros_like(my_tiles))
    onehot = (
        (columns[:, None] == jnp.arange(nrows, dtype=jnp.int32)[None, :]) & live[:, None]
    ).astype(jnp.bfloat16)
    outgoing = jnp.einsum(
        "sc,sij->cij", onehot, my_tiles, preferred_element_type=jnp.float32
    ).astype(jnp.bfloat16)
    incoming = lax.all_to_all(outgoing, "rows", split_axis=0, concat_axis=0, tiled=True)
    current = start_right[0]
    whole = lax.all_gather(current, "rows", axis=0, tiled=True)
    picked = whole.reshape(nrows, BLOCK, COLS)[columns]
    partial_value = jnp.einsum("sij,sjk->ik", masked, picked, preferred_element_type=jnp.float32)
    summed = lax.psum(partial_value, "tm")
    gram = lax.psum(gram_of(summed), "rows")
    left_embed = orthonormal(summed, gram, nodes)
    basis = lax.all_gather(left_embed.astype(jnp.bfloat16), "rows", axis=0, tiled=True)
    image = jnp.einsum(
        "rij,rik->jk",
        incoming,
        basis.reshape(nrows, BLOCK, COLS),
        preferred_element_type=jnp.float32,
    )
    rgram = lax.psum(gram_of(image), ("tm", "rows"))
    right_embed = orthonormal(image, rgram, nodes * nsnaps)
    return (left_embed, right_embed[None])


def solution(mesh):
    placed = (P("tm", "rows", None, None), P("tm", "rows"), P("tm", "rows"), P("tm", "rows", None))
    return jax.shard_map(
        on_device,
        mesh=mesh,
        in_specs=placed,
        out_specs=(P("rows", None), P("tm", "rows", None)),
        check_vma=False,
    )
```

profile of v0, /device:TPU:0, one launch (start us, length us, event | category | flops | bytes accessed | tf_op | source)
XLA Modules:
  0.0 516.3 jit_solution(13948619918923073705)
XLA Ops:
  9.3 59.5 %all-gather.6.cloned.1.call-done = bf16[1,2048,256]{2,1,0:T(8,128)(2,1)} async-done(((bf16[1,128,256]{2,1,0:T(8,128)(2,1)}), bf16[1,2048,256]{2,1,0:T(8,128)(2,1)}) %all-gather.6.cloned.1.call-update) | async-done | bytes 1048592 | tf_op jit(solution)/shard_map/all_gather | solution.py:40
  68.8 1.8 gather_fusion
  71.6 16.8 %all-reduce.5.cloned.1.call-done = f32[128,256]{1,0:T(8,128)} async-done(((f32[128,256]{1,0:T(8,128)}), f32[128,256]{1,0:T(8,128)}) %all-reduce.5.cloned.1.call-update) | async-done | bytes 131088 | tf_op jit(solution)/shard_map/psum | solution.py:43
  88.5 2.1 fusion.33
  90.6 111.0 %all-reduce.7.cloned.1.call-done = f32[256,256]{0,1:T(8,128)} async-done(((f32[256,256]{0,1:T(8,128)}), f32[256,256]{0,1:T(8,128)}) %all-reduce.7.cloned.1.call-update) | async-done | bytes 262160 | tf_op jit(solution)/shard_map/psum | solution.py:44
  202.8 11.7 %cholesky.130 = f32[128,128]{1,0:T(8,128)S(1)} custom-call(f32[128,128]{1,0:T(8,128)S(1)} %cholesky.194), custom_call_target="Cholesky" | custom-call | tf_op jit(solution)/shard_map/jit(cholesky)/cholesky | solution.py:12
  214.6 9.8 %custom-call.13 = f32[1,128,128]{1,2,0:T(8,128)S(1)} custom-call(f32[1,128,128]{2,1,0:T(8,128)S(1)} %get-tuple-element.51), custom_call_target="InvertDiagBlocksLowerTriangular" | custom-call | tf_op jit(solution)/shard_map/jit(cholesky)/cholesky | solution.py:12
  224.9 11.7 %cholesky.147 = f32[128,128]{1,0:T(8,128)S(1)} custom-call(f32[128,128]{1,0:T(8,128)S(1)} %convolution_subtract_fusion.3), custom_call_target="Cholesky" | custom-call | tf_op jit(solution)/shard_map/jit(cholesky)/cholesky | solution.py:12
  238.8 4.2 while.4
  239.5 1.4 bitcast_dynamic-update-slice_fusion.4
  241.5 1.4 bitcast_dynamic-update-slice_fusion.4
  242.9 19.7 %custom-call.14 = f32[2,128,128]{1,2,0:T(8,128)S(1)} custom-call(f32[2,128,128]{2,1,0:T(8,128)S(1)} %get-tuple-element.18), custom_call_target="InvertDiagBlocksLowerTriangular" | custom-call | tf_op jit(solution)/shard_map/triangular_solve/custom-call.0 | solution.py:13
  264.6 1.2 copy.15
  265.8 4.6 all-to-all-start
  270.5 45.9 %all-gather.4.cloned.1.call-done = bf16[2048,256]{0,1:T(8,128)(2,1)} async-done(((bf16[128,256]{0,1:T(8,128)(2,1)}), bf16[2048,256]{0,1:T(8,128)(2,1)}) %all-gather.4.cloned.1.call-update) | async-done | bytes 1048592 | tf_op jit(solution)/shard_map/all_gather | solution.py:46
  316.4 1.5 copy.17
  320.1 126.4 %all-reduce.9.cloned.1.call-done = f32[256,256]{0,1:T(8,128)} async-done(((f32[256,256]{0,1:T(8,128)}), f32[256,256]{0,1:T(8,128)}) %all-reduce.9.cloned.1.call-update) | async-done | bytes 262160 | tf_op jit(solution)/shard_map/psum | solution.py:53
  447.7 11.7 %cholesky.164 = f32[128,128]{1,0:T(8,128)S(1)} custom-call(f32[128,128]{1,0:T(8,128)S(1)} %cholesky.197), custom_call_target="Cholesky" | custom-call | tf_op jit(solution)/shard_map/jit(cholesky)/cholesky | solution.py:12
  459.5 9.8 %custom-call.15 = f32[1,128,128]{1,2,0:T(8,128)S(1)} custom-call(f32[1,128,128]{2,1,0:T(8,128)S(1)} %get-tuple-element.47), custom_call_target="InvertDiagBlocksLowerTriangular" | custom-call | tf_op jit(solution)/shard_map/jit(cholesky)/cholesky | solution.py:12
  469.8 11.7 %cholesky.181 = f32[128,128]{1,0:T(8,128)S(1)} custom-call(f32[128,128]{1,0:T(8,128)S(1)} %convolution_subtract_fusion.1), custom_call_target="Cholesky" | custom-call | tf_op jit(solution)/shard_map/jit(cholesky)/cholesky | solution.py:12
  484.2 4.0 while.5
  484.8 1.4 bitcast_dynamic-update-slice_fusion.5
  486.8 1.4 bitcast_dynamic-update-slice_fusion.5
  488.2 19.9 %custom-call.16 = f32[2,128,128]{1,2,0:T(8,128)S(1)} custom-call(f32[2,128,128]{2,1,0:T(8,128)S(1)} %get-tuple-element.19), custom_call_target="InvertDiagBlocksLowerTriangular" | custom-call | tf_op jit(solution)/shard_map/triangular_solve/custom-call.0 | solution.py:13
  (71 shorter events, 16.3 us)
Async XLA Ops:
  7.2 61.6 %all-gather.6.cloned.1.call-start = ((), (), s32[]{:S(2)}) async-start(), calls=%async_computation.5 | async-start | bytes 1114112 | tf_op jit(solution)/shard_map/all_gather | solution.py:40
  7.9 80.6 %all-reduce.5.cloned.1.call-start = ((), (), s32[]{:S(2)}) async-start(), calls=%async_computation.1 | async-start | bytes 262144 | tf_op jit(solution)/shard_map/psum | solution.py:43
  8.6 0.7 copy-start.4
  68.8 1.9 copy-start.1
  71.6 130.0 %all-reduce.7.cloned.1.call-start = ((), (), s32[]{:S(2)}) async-start(), calls=%async_computation.2 | async-start | bytes 524288 | tf_op jit(solution)/shard_map/psum | solution.py:44
  90.6 225.8 %all-gather.4.cloned.1.call-start = ((), (), s32[]{:S(2)}) async-start(), calls=%async_computation.3 | async-start | bytes 1114112 | tf_op jit(solution)/shard_map/all_gather | solution.py:46
  201.6 1.2 copy-start.2
  238.7 23.9 %copy-start = (f32[128,256]{1,0:T(8,128)S(1)}, f32[128,256]{1,0:T(8,128)}, u32[]{:S(2)}) copy-start(f32[128,256]{1,0:T(8,128)} %all-reduce.5.cloned.1.call-done) | copy-start | bytes 393220
  265.8 52.0 %all-to-all-start = ((bf16[16,128,128]{1,2,0:T(8,128)(2,1)}), bf16[16,128,128]{1,2,0:T(8,128)(2,1)S(1)}, u32[]{:S(2)}, u32[]{:S(2)}) async-start(bf16[16,128,128]{1,2,0:T(8,128)(2,1)} %copy.15), calls=%async_computation | async-start | bytes 1048576 | tf_op jit(solution)/shard_map/all_to_all | solution.py:38
  270.5 176.0 %all-reduce.9.cloned.1.call-start = ((), (), s32[]{:S(2)}) async-start(), calls=%async_computation.4 | async-start | bytes 524288 | tf_op jit(solution)/shard_map/psum | solution.py:53
  446.5 1.2 copy-start.3
Sparse Core Ops, SparseCore 0:
  10.8 57.9 all-gather.5
  71.7 16.7 all-reduce.4
  93.7 107.8 all-reduce.6
  264.3 52.0 all-gather.3
  322.7 123.8 all-reduce.8
where the time goes:
time: 517 us; the launch traced here: 516 us
  waiting for transfers between devices  360 us (70%)
  other arithmetic  109 us (21%)
  between operations  17.3 us (3%)
  local copies, waits for them, and re-layouts  17 us (3%)
  matrix products  7.52 us (1%)
    psum x1, waiting for transfers between devices, on_device(): rgram = lax.psum(gram_of(image), ('tm', 'rows'))  126 us
    psum x1, waiting for transfers between devices, on_device(): gram = lax.psum(gram_of(summed), 'rows')  111 us
    another operation x13, other arithmetic, orthonormal(): factor = jnp.linalg.cholesky(gram)  68.6 us
    all_gather x1, waiting for transfers between devices, on_device(): whole = lax.all_gather(current, 'rows', axis=0, tiled=True)  59.5 us
    all_gather x1, waiting for transfers between devices, on_device(): lax.all_gather(left_embed.astype(jnp.bfloat16), 'rows', axis=0, tiled=True)  45.9 us
    another operation x5, other arithmetic, orthonormal(): lax.linalg.triangular_solve(factor, values, left_side=False, lower=True,...  39.6 us
    psum x1, waiting for transfers between devices, on_device(): summed = lax.psum(partial_value, 'tm')  16.8 us
  transfers between devices with their start and end apart: 6, of which 5 were waited for; matrix products, arithmetic and copies ran while one was open for 1% of the time, Pallas kernels for 0%

commit v1 on v0

--- a/solution.py
+++ b/solution.py
@@ -50,7 +50,9 @@
         basis.reshape(nrows, BLOCK, COLS),
         preferred_element_type=jnp.float32,
     )
-    rgram = lax.psum(gram_of(image), ("tm", "rows"))
+    own = gram_of(image)
+    terms = lax.all_gather(own, ("tm", "rows"))
+    rgram = jnp.sum(terms, axis=0)
     right_embed = orthonormal(image, rgram, nodes * nsnaps)
     return (left_embed, right_embed[None])
 

time: 517 us -> 474 us (0.917)
  waiting for transfers between devices: 360 us -> 309 us
  other arithmetic: 109 us -> 115 us
    psum x1 -> x0, waiting for transfers between devices: 126 us -> none  [on_device(): rgram = lax.psum(gram_of(image), ('tm', 'rows'))]
    all_gather x0 -> x1, waiting for transfers between devices: none -> 75.9 us  [on_device(): terms = lax.all_gather(own, ('tm', 'rows'))]
where the time goes in v1:
time: 474 us; the launch traced here: 473 us
  waiting for transfers between devices  309 us (65%)
  other arithmetic  115 us (24%)
  between operations  17.4 us (4%)
  local copies, waits for them, and re-layouts  15.5 us (3%)
  matrix products  11.1 us (2%)
  starting transfers between devices  4.83 us (1%)
    psum x1, waiting for transfers between devices, on_device(): gram = lax.psum(gram_of(summed), 'rows')  111 us
    all_gather x1, waiting for transfers between devices, on_device(): terms = lax.all_gather(own, ('tm', 'rows'))  75.9 us
    another operation x13, other arithmetic, orthonormal(): factor = jnp.linalg.cholesky(gram)  68.7 us
    all_gather x1, waiting for transfers between devices, on_device(): whole = lax.all_gather(current, 'rows', axis=0, tiled=True)  59.5 us
    all_gather x1, waiting for transfers between devices, on_device(): lax.all_gather(left_embed.astype(jnp.bfloat16), 'rows', axis=0, tiled=True)  45.1 us
    another operation x5, other arithmetic, orthonormal(): lax.linalg.triangular_solve(factor, values, left_side=False, lower=True,...  39.6 us
    psum x1, waiting for transfers between devices, on_device(): summed = lax.psum(partial_value, 'tm')  16.8 us
  transfers between devices with their start and end apart: 6, of which 5 were waited for; matrix products, arithmetic and copies ran while one was open for 1% of the time, Pallas kernels for 0%

profile of v1, /device:TPU:0, one launch (start us, length us, event | category | flops | bytes accessed | tf_op | source)
XLA Modules:
  0.0 472.8 jit_solution(2501527382287820364)
XLA Ops:
  9.3 59.5 %all-gather.8.cloned.1.call-done = bf16[1,2048,256]{2,1,0:T(8,128)(2,1)} async-done(((bf16[1,128,256]{2,1,0:T(8,128)(2,1)}), bf16[1,2048,256]{2,1,0:T(8,128)(2,1)}) %all-gather.8.cloned.1.call-update) | async-done | bytes 1048592 | tf_op jit(solution)/shard_map/all_gather | solution.py:40
  68.8 1.8 gather_fusion
  70.6 1.9 convolution_bitcast_fusion
  72.5 16.8 %all-reduce.4.cloned.1.call-done = f32[128,256]{1,0:T(8,128)} async-done(((f32[128,256]{1,0:T(8,128)}), f32[128,256]{1,0:T(8,128)}) %all-reduce.4.cloned.1.call-update) | async-done | bytes 131088 | tf_op jit(solution)/shard_map/psum | solution.py:43
  89.4 2.1 fusion.33
  91.5 111.0 %all-reduce.6.cloned.1.call-done = f32[256,256]{0,1:T(8,128)} async-done(((f32[256,256]{0,1:T(8,128)}), f32[256,256]{0,1:T(8,128)}) %all-reduce.6.cloned.1.call-update) | async-done | bytes 262160 | tf_op jit(solution)/shard_map/psum | solution.py:44
  204.7 11.7 %cholesky.130 = f32[128,128]{1,0:T(8,128)S(1)} custom-call(f32[128,128]{1,0:T(8,128)S(1)} %cholesky.194), custom_call_target="Cholesky" | custom-call | tf_op jit(solution)/shard_map/jit(cholesky)/cholesky | solution.py:12
  216.4 9.8 %custom-call.13 = f32[1,128,128]{1,2,0:T(8,128)S(1)} custom-call(f32[1,128,128]{2,1,0:T(8,128)S(1)} %get-tuple-element.53), custom_call_target="InvertDiagBlocksLowerTriangular" | custom-call | tf_op jit(solution)/shard_map/jit(cholesky)/cholesky | solution.py:12
  226.7 11.7 %cholesky.147 = f32[128,128]{1,0:T(8,128)S(1)} custom-call(f32[128,128]{1,0:T(8,128)S(1)} %convolution_subtract_fusion.3), custom_call_target="Cholesky" | custom-call | tf_op jit(solution)/shard_map/jit(cholesky)/cholesky | solution.py:12
  240.7 4.3 while.4
  241.5 1.4 bitcast_dynamic-update-slice_fusion.4
  243.5 1.4 bitcast_dynamic-update-slice_fusion.4
  245.0 19.7 %custom-call.14 = f32[2,128,128]{1,2,0:T(8,128)S(1)} custom-call(f32[2,128,128]{2,1,0:T(8,128)S(1)} %get-tuple-element.18), custom_call_target="InvertDiagBlocksLowerTriangular" | custom-call | tf_op jit(solution)/shard_map/triangular_solve/custom-call.0 | solution.py:13
  270.5 4.6 all-to-all-start
  275.2 45.1 %all-gather.6.cloned.1.call-done = bf16[2048,256]{0,1:T(8,128)(2,1)} async-done(((bf16[128,256]{0,1:T(8,128)(2,1)}), bf16[2048,256]{0,1:T(8,128)(2,1)}) %all-gather.6.cloned.1.call-update) | async-done | bytes 1048592 | tf_op jit(solution)/shard_map/all_gather | solution.py:46
  320.3 1.5 copy.21
  324.0 75.9 %all-gather.10.cloned.1.call-done = f32[8192,256]{1,0:T(8,128)} async-done(((f32[256,256]{1,0:T(8,128)}), f32[8192,256]{1,0:T(8,128)}) %all-gather.10.cloned.1.call-update) | async-done | bytes 8388624 | tf_op jit(solution)/shard_map/all_gather | solution.py:54
  399.9 3.9 reduce_sum.9
  404.1 11.7 %cholesky.164 = f32[128,128]{1,0:T(8,128)S(1)} custom-call(f32[128,128]{1,0:T(8,128)S(1)} %cholesky.197), custom_call_target="Cholesky" | custom-call | tf_op jit(solution)/shard_map/jit(cholesky)/cholesky | solution.py:12
  415.8 9.8 %custom-call.15 = f32[1,128,128]{1,2,0:T(8,128)S(1)} custom-call(f32[1,128,128]{2,1,0:T(8,128)S(1)} %get-tuple-element.49), custom_call_target="InvertDiagBlocksLowerTriangular" | custom-call | tf_op jit(solution)/shard_map/jit(cholesky)/cholesky | solution.py:12
  426.1 11.7 %cholesky.181 = f32[128,128]{1,0:T(8,128)S(1)} custom-call(f32[128,128]{1,0:T(8,128)S(1)} %convolution_subtract_fusion.1), custom_call_target="Cholesky" | custom-call | tf_op jit(solution)/shard_map/jit(cholesky)/cholesky | solution.py:12
  440.6 4.1 while.5
  441.2 1.4 bitcast_dynamic-update-slice_fusion.5
  444.7 19.9 %custom-call.16 = f32[2,128,128]{1,2,0:T(8,128)S(1)} custom-call(f32[2,128,128]{2,1,0:T(8,128)S(1)} %get-tuple-element.19), custom_call_target="InvertDiagBlocksLowerTriangular" | custom-call | tf_op jit(solution)/shard_map/triangular_solve/custom-call.0 | solution.py:13
  (62 shorter events, 20.7 us)
Async XLA Ops:
  7.2 61.6 %all-gather.8.cloned.1.call-start = ((), (), s32[]{:S(2)}) async-start(), calls=%async_computation.4 | async-start | bytes 1114112 | tf_op jit(solution)/shard_map/all_gather | solution.py:40
  7.9 81.5 %all-reduce.4.cloned.1.call-start = ((), (), s32[]{:S(2)}) async-start(), calls=%async_computation.1 | async-start | bytes 262144 | tf_op jit(solution)/shard_map/psum | solution.py:43
  72.5 130.1 %all-reduce.6.cloned.1.call-start = ((), (), s32[]{:S(2)}) async-start(), calls=%async_computation.2 | async-start | bytes 524288 | tf_op jit(solution)/shard_map/psum | solution.py:44
  91.5 228.9 %all-gather.6.cloned.1.call-start = ((), (), s32[]{:S(2)}) async-start(), calls=%async_computation.3 | async-start | bytes 1114112 | tf_op jit(solution)/shard_map/all_gather | solution.py:46
  270.5 51.3 %all-to-all-start = ((bf16[16,128,128]{1,2,0:T(8,128)(2,1)}), bf16[16,128,128]{1,2,0:T(8,128)(2,1)S(1)}, u32[]{:S(2)}, u32[]{:S(2)}) async-start(bf16[16,128,128]{1,2,0:T(8,128)(2,1)} %copy.20), calls=%async_computation | async-start | bytes 1048576 | tf_op jit(solution)/shard_map/all_to_all | solution.py:38
  275.2 124.8 %all-gather.10.cloned.1.call-start = ((), (), s32[]{:S(2)}) async-start(), calls=%async_computation.5 | async-start | bytes 8650752 | tf_op jit(solution)/shard_map/all_gather | solution.py:54
Sparse Core Ops, SparseCore 0:
  10.8 57.9 all-gather.7
  72.6 16.7 all-reduce.3
  94.6 107.9 all-reduce.5
  268.0 52.2 all-gather.5
  323.5 76.4 all-gather.9
